TPU v7x, 256 devices: a whole 4x4x8 slice. The times are simulated.
256 devices in a mesh: gx: 32 (over y, z_lo, x), gy: 8 (over z_hi, core).
Axes of the slice: x: 4, y: 4, z: 8 (z_hi: 4, z_lo: 2; z = z_hi * 2 + z_lo), core: 2. Of those that a mesh axis runs over, the one named last changes fastest.
Arguments:
- hidden: bfloat16 [2240, 5120], P('gy', 'gx'), may hold values from -6 to 6
- norm_gain: float32 [5120], P('gx'), may hold values from 0.1 to 1.9
- qkv_weight: bfloat16 [5120, 7168], P('gx', 'gy'), may hold values from -0.078125 to 0.078125
- qkv_bias: bfloat16 [7168], P('gy'), may hold values from -5 to 5
- out_weight: bfloat16 [5120, 5120], P('gy', 'gx'), may hold values from -0.078125 to 0.078125
- key_cache: bfloat16 [5, 8704, 1024], P(None, 'gx', 'gy'), may hold values from -68 to 68
- value_cache: bfloat16 [5, 8704, 1024], P(None, 'gx', 'gy'), may hold values from -12 to 12
- cached_len: int32 [5], replicated, may hold values from 1 to 8192, as said below
- fresh_len: int32 [5], replicated, may hold values from 224 to 448, as said below
Outputs:
- output: bfloat16 [2240, 5120], P('gy', 'gx')
- key_out: bfloat16 [5, 8704, 1024], P(None, 'gx', 'gy')
- value_out: bfloat16 [5, 8704, 1024], P(None, 'gx', 'gy')
Inputs may be any that keep to these rules, and one draw needn't show every extreme that they name: `cached_len`: two requests have 8192 - 8192 // 32 or more cached tokens, one of them exactly 8192; the other three fewer than 256. `fresh_len`: one request has exactly 448 live new tokens.
All inputs are finite; a program needn't handle non-finite values.
Results may differ from a plain program's by a relative error of at most 0.012.
Values may be sent and summed in bfloat16 or wider, within the bound.
A program may use at most 128 MiB of HBM per device.

v0:
```python
import jax
import jax.numpy as jnp
from jax import lax
from jax.sharding import Mesh
from jax.sharding import PartitionSpec as P

HEAD_DIM = 128
GROUP = 5
REQUESTS = 5
NEW_TOKENS = 448
ROPE_THETA = 1000000.0
NORM_EPS = 1e-06
NEG_LARGE = -1e30


def rotate(vectors, positions):
    half_dim = vectors.shape[-1] // 2
    exponent = jnp.arange(half_dim, dtype=jnp.int32).astype(jnp.float32) * (2.0 / vectors.shape[-1])
    frequency = 1.0 / ROPE_THETA**exponent
    angles = positions[:, None] * frequency[None, :]
    target = (positions.shape[0],) + (1,) * (vectors.ndim - 2) + (half_dim,)
    cos_table = jnp.cos(angles).reshape(target)
    sin_table = jnp.sin(angles).reshape(target)
    first_half = vectors[..., :half_dim]
    second_half = vectors[..., half_dim:]
    return jnp.concatenate(
        [
            first_half * cos_table - second_half * sin_table,
            second_half * cos_table + first_half * sin_table,
        ],
        -1,
    )


def token_positions(cached_len, fresh_len, first_row, row_count):
    rows_here = first_row + jnp.arange(row_count, dtype=jnp.int32)
    request = rows_here // NEW_TOKENS
    within = rows_here % NEW_TOKENS
    picked = request[:, None] == jnp.arange(REQUESTS, dtype=jnp.int32)[None, :]
    start_pos = jnp.sum(jnp.where(picked, cached_len[None, :], 0), 1)
    live_count = jnp.sum(jnp.where(picked, fresh_len[None, :], 0), 1)
    return (start_pos + within, within < live_count)


def finish_rows(projected, cached_len, fresh_len, first_row):
    row_count = projected.shape[0]
    groups_here = projected.shape[1] // ((GROUP + 2) * HEAD_DIM)
    shaped = projected.reshape(row_count, groups_here, GROUP + 2, HEAD_DIM)
    positions, unused_live = token_positions(cached_len, fresh_len, first_row, row_count)
    angle_pos = positions.astype(jnp.float32)
    queries = rotate(shaped[:, :, :GROUP], angle_pos).astype(jnp.bfloat16).reshape(row_count, -1)
    new_keys = rotate(shaped[:, :, GROUP], angle_pos).astype(jnp.bfloat16).reshape(row_count, -1)
    new_values = shaped[:, :, GROUP + 1].astype(jnp.bfloat16).reshape(row_count, -1)
    return (queries, new_keys, new_values)


def append_rows(cache, new_rows, cached_len, fresh_len, first_slot):
    slot_count = cache.shape[1]
    slot_pos = first_slot + jnp.arange(slot_count, dtype=jnp.int32)
    offsets = slot_pos[None, :] - cached_len[:, None]
    is_live = (offsets >= 0) & (offsets < fresh_len[:, None])
    source_rows = jnp.arange(REQUESTS, dtype=jnp.int32)[:, None] * NEW_TOKENS + jnp.clip(
        offsets, 0, NEW_TOKENS - 1
    )
    return jnp.where(is_live[:, :, None], jnp.take(new_rows, source_rows, axis=0), cache)


GX = ("y", "zl", "x")
GY = ("zh", "c")


def gather_gx(value):
    for axis in GX[::-1]:
        value = lax.all_gather(value, axis, axis=0, tiled=True)
    return value


def psum_gx(value):
    for axis in GX[::-1]:
        value = lax.psum(value, axis)
    return value


def pmax_gx(value):
    for axis in GX[::-1]:
        value = lax.pmax(value, axis)
    return value


def share_rows(share_sum, cached_len, fresh_len, first_row):
    queries, new_keys, new_values = finish_rows(share_sum, cached_len, fresh_len, first_row)
    widths = (queries.shape[1], new_keys.shape[1])
    joined = gather_gx(jnp.concatenate([queries, new_keys, new_values], axis=1))
    return (
        joined[:, : widths[0]],
        joined[:, widths[0] : widths[0] + widths[1]],
        joined[:, widths[0] + widths[1] :],
    )


def per_device(
    hidden,
    norm_gain,
    qkv_weight,
    qkv_bias,
    out_weight,
    key_cache,
    value_cache,
    cached_len,
    fresh_len,
):
    scale = HEAD_DIM ** (-0.5)
    token_count = REQUESTS * NEW_TOKENS
    gx_size = lax.psum(1, GX)
    model_width = hidden.shape[1] * gx_size
    hidden_f = hidden.astype(jnp.float32)
    squares = psum_gx(jnp.sum(hidden_f * hidden_f, axis=1))
    normed = (
        hidden_f * lax.rsqrt(squares / model_width + NORM_EPS)[:, None] * norm_gain[None, :]
    ).astype(jnp.bfloat16)
    gathered = lax.all_gather(normed, GY, axis=0, tiled=True)
    bias_f = qkv_bias.astype(jnp.float32)[None, :]
    row_share = token_count // gx_size
    share_start = lax.axis_index(GX) * row_share
    summed = lax.psum_scatter(
        jnp.dot(gathered, qkv_weight, preferred_element_type=jnp.float32),
        GX,
        scatter_dimension=0,
        tiled=True,
    )
    queries, new_keys, new_values = share_rows(summed + bias_f, cached_len, fresh_len, share_start)
    slot_count = key_cache.shape[1]
    first_slot = lax.axis_index(GX) * slot_count
    key_out = append_rows(key_cache, new_keys, cached_len, fresh_len, first_slot)
    value_out = append_rows(value_cache, new_values, cached_len, fresh_len, first_slot)
    groups_here = key_cache.shape[2] // HEAD_DIM
    query_blocks = queries.reshape(REQUESTS, NEW_TOKENS, groups_here, GROUP, HEAD_DIM)
    key_blocks = key_out.reshape(REQUESTS, slot_count, groups_here, HEAD_DIM)
    value_blocks = value_out.reshape(REQUESTS, slot_count, groups_here, HEAD_DIM)
    slot_pos = first_slot + jnp.arange(slot_count, dtype=jnp.int32)
    query_pos = jnp.arange(NEW_TOKENS, dtype=jnp.int32)

    def visible_for(cached_here, fresh_here):
        return (slot_pos[None, :] < cached_here + fresh_here) & (
            slot_pos[None, :] <= cached_here + query_pos[:, None]
        )

    def scores_for(query_req, key_req, visible):
        scores = (
            jnp.einsum("ikgd,pkd->kgip", query_req, key_req, preferred_element_type=jnp.float32)
            * scale
        )
        return jnp.where(visible[None, None], scores, NEG_LARGE)

    def local_top(items):
        query_req, key_req, cached_here, fresh_here = items
        return jnp.max(scores_for(query_req, key_req, visible_for(cached_here, fresh_here)), axis=3)

    highest = lax.map(local_top, (query_blocks, key_blocks, cached_len, fresh_len))
    highest = pmax_gx(highest.astype(jnp.bfloat16)).astype(highest.dtype)

    def local_sums(items):
        query_req, key_req, value_req, cached_here, fresh_here, top_here = items
        visible = visible_for(cached_here, fresh_here)
        scores = scores_for(query_req, key_req, visible)
        weighted = jnp.where(visible[None, None], jnp.exp(scores - top_here[..., None]), 0.0)
        denom = jnp.sum(weighted, axis=3)
        mixed = jnp.einsum(
            "kgip,pkd->ikgd",
            weighted.astype(jnp.bfloat16),
            value_req,
            preferred_element_type=jnp.float32,
        )
        return (mixed.reshape(NEW_TOKENS, -1), denom.reshape(-1, NEW_TOKENS).T)

    mixed, denom = lax.map(
        local_sums, (query_blocks, key_blocks, value_blocks, cached_len, fresh_len, highest)
    )
    mixed = mixed.reshape(token_count, -1)
    denom = denom.reshape(token_count, -1)
    mixed_width = mixed.shape[1]
    pad = jnp.zeros((token_count, HEAD_DIM - denom.shape[1]), jnp.float32)
    both = jnp.concatenate([mixed, denom, pad], axis=1).astype(jnp.bfloat16)
    both = lax.psum_scatter(both, GX, scatter_dimension=0, tiled=True).astype(jnp.float32)
    mixed = both[:, :mixed_width]
    denom = both[:, mixed_width : mixed_width + denom.shape[1]]
    unused_pos, is_live = token_positions(cached_len, fresh_len, share_start, row_share)
    ratio = mixed.reshape(row_share, -1, HEAD_DIM) / denom[:, :, None]
    attended = jnp.where(is_live[:, None], ratio.reshape(row_share, -1), 0.0).astype(jnp.bfloat16)
    partial_out = jnp.dot(gather_gx(attended), out_weight, preferred_element_type=jnp.float32)
    summed_out = lax.psum_scatter(
        partial_out.astype(jnp.bfloat16), GY, scatter_dimension=0, tiled=True
    ).astype(jnp.float32)
    output = (hidden_f + summed_out).astype(jnp.bfloat16)
    return (output, key_out, value_out)


def solution(mesh):
    sub_mesh = Mesh(
        mesh.devices.reshape(4, mesh.shape["gx"] // 16, 4, mesh.shape["gy"] // 2, 2), GX + GY
    )
    in_specs = (
        P(GY, GX),
        P(GX),
        P(GX, GY),
        P(GY),
        P(GY, GX),
        P(None, GX, GY),
        P(None, GX, GY),
        P(),
        P(),
    )
    out_specs = (P(GY, GX), P(None, GX, GY), P(None, GX, GY))
    return jax.shard_map(
        per_device, mesh=sub_mesh, in_specs=in_specs, out_specs=out_specs, check_vma=False
    )
```

profile of v0, /device:TPU:10, one launch (start us, length us, event | category | flops | bytes accessed | tf_op | source)
XLA Modules:
  0.0 617.7 jit_solution(14488319229614992455)
XLA Ops:
  8.2 8.6 %psum.21 = f32[280]{0:T(512)S(1)} all-reduce(f32[280]{0:T(512)S(1)} %fusion.40), channel_id=1, replica_groups=mesh['y'=4,'zl'=2,'x'=4,'zh'=4,'c'=2] {'x'}, use_global_device_ids=true, to_apply=%region_2.0 | all-reduce | flops 280 | bytes 2240 | tf_op jit(solution)/shard_map/psum | solution.py:80
  16.8 4.9 psum.22
  21.7 9.5 %psum.23 = f32[280]{0:T(512)S(1)} all-reduce(f32[280]{0:T(512)S(1)} %psum.22), channel_id=1, replica_groups=mesh['y'=4,'zl'=2,'x'=4,'zh'=4,'c'=2] {'y'}, use_global_device_ids=true, to_apply=%region_4.0 | all-reduce | flops 280 | bytes 2240 | tf_op jit(solution)/shard_map/psum | solution.py:80
  32.2 19.2 %all-gather = bf16[8,280,160]{1,2,0:T(8,128)(2,1)S(1)} all-gather(bf16[1,280,160]{1,2,0:T(8,128)(2,1)S(1)} %fusion.46), channel_id=1, replica_groups=mesh['y'=4,'zl'=2,'x'=4,'zh'=4,'c'=2] {'zh','c'}, dimensions={0}, use_global_device_ids=true | all-gather | bytes 806400 | tf_op jit(solution)/shard_map/all_gather | solution.py:121
  52.5 4.5 fusion.63
  57.0 115.8 %fusion.8 = f32[80,896]{1,0:T(8,128)S(1)} fusion(f32[2240,896]{1,0:T(8,128)} %fusion.63), kind=kCustom, calls=%all-reduce-scatter | all-reduce-scatter fusion | flops 2293761 | bytes 8315904
  178.4 5.2 collective-permute-start.2
  189.4 8.7 %collective-permute-done.3 = f32[70,896]{1,0:T(8,128)S(1)} collective-permute-done((f32[70,896]{1,0:T(8,128)S(1)}, f32[70,896]{1,0:T(8,128)S(1)}, u32[]{:S(2)}, u32[]{:S(2)}) %collective-permute-start.3) | collective-permute-done | bytes 250912
  200.4 14.4 %all-gather.1 = bf16[4,70,896]{2,1,0:T(8,128)(2,1)S(1)} all-gather(bf16[1,70,896]{2,1,0:T(8,128)(2,1)S(1)} %maximum_bitcast_fusion.1), channel_id=1, replica_groups=mesh['y'=4,'zl'=2,'x'=4,'zh'=4,'c'=2] {'x'}, dimensions={0}, use_global_device_ids=true | all-gather | bytes 627200 | tf_op jit(solution)/shard_map/all_gather | solution.py:74
  215.0 9.7 %all_gather.23 = bf16[560,896]{1,0:T(8,128)(2,1)} all-gather(bf16[280,896]{1,0:T(8,128)(2,1)S(1)} %reshape.471), channel_id=1, replica_groups=mesh['y'=4,'zl'=2,'x'=4,'zh'=4,'c'=2] {'zl'}, dimensions={0}, use_global_device_ids=true | all-gather | bytes 1505280 | tf_op jit(solution)/shard_map/all_gather | solution.py:74
  225.1 46.4 %all-gather.6.cloned.1.call-done = bf16[2240,896]{1,0:T(8,128)(2,1)} async-done(((bf16[560,896]{1,0:T(8,128)(2,1)}), bf16[2240,896]{1,0:T(8,128)(2,1)}) %all-gather.6.cloned.1.call-update) | async-done | bytes 4014096 | tf_op jit(solution)/shard_map/all_gather | solution.py:74
  273.3 5.2 reshape.445
  278.5 4.8 copy.68
  290.7 24.8 %while.24 = (s32[]{:T(128)}, bf16[5,1,5,448]{3,2,1,0:T(8,128)(2,1)S(1)}, s32[5]{0:T(128)S(1)}, s32[5]{0:T(128)S(1)}, bf16[5,272,1,128]{3,1,2,0:T(8,128)(2,1)S(1)...) while((s32[]{:T(128)}, bf16[5,1,5,448]{3,2,1,0:T(8,128)(2,1)S(1)}, ...), condition=%wide.region_9.11_spmd.clone, body=%wide.region_7.10_spmd.clone.sunk | while | flops 158046256 | bytes 932525 | solution.py:159
  315.5 14.4 %pmax.21 = bf16[5,1,5,448]{3,2,1,0:T(8,128)(2,1)S(1)} all-reduce(bf16[5,1,5,448]{3,2,1,0:T(8,128)(2,1)S(1)} %get-tuple-element.104), channel_id=1, replica_groups=mesh['y'=4,'zl'=2,'x'=4,'zh'=4,'c'=2] {'x'}, use_global_device_ids=true, to_apply=%region_10.12 | all-reduce | flops 11200 | bytes 44800 | tf_op jit(solution)/shard_map/pmax | solution.py:86
  329.9 8.5 %pmax.22 = bf16[5,1,5,448]{3,2,1,0:T(8,128)(2,1)S(1)} all-reduce(bf16[5,1,5,448]{3,2,1,0:T(8,128)(2,1)S(1)} %pmax.21), channel_id=1, replica_groups=mesh['y'=4,'zl'=2,'x'=4,'zh'=4,'c'=2] {'zl'}, use_global_device_ids=true, to_apply=%region_11.13 | all-reduce | flops 11200 | bytes 44800 | tf_op jit(solution)/shard_map/pmax | solution.py:86
  338.5 14.7 %pmax.23 = bf16[5,1,5,448]{3,2,1,0:T(8,128)(2,1)S(1)} all-reduce(bf16[5,1,5,448]{3,2,1,0:T(8,128)(2,1)S(1)} %pmax.22), channel_id=1, replica_groups=mesh['y'=4,'zl'=2,'x'=4,'zh'=4,'c'=2] {'y'}, use_global_device_ids=true, to_apply=%region_12.14 | all-reduce | flops 11200 | bytes 44800 | tf_op jit(solution)/shard_map/pmax | solution.py:86
  353.2 38.3 %while.25 = (s32[]{:T(128)}, bf16[5,448,640]{1,2,0:T(8,128)(2,1)}, bf16[5,448,5]{1,2,0:T(8,128)(2,1)S(1)}, bf16[5,272,1,128]{3,1,2,0:T(8,128)(2,1)S(1)}, s32[5]{...) while((s32[]{:T(128)}, bf16[5,448,640]{1,2,0:T(8,128)(2,1)}, ...), condition=%wide.region_15.17_spmd.clone, body=%wide.region_13.16_spmd.clone.sunk | while | flops 318286912 | bytes 9364173 | solution.py:176
  392.3 4.3 copy.69
  401.2 88.4 %fusion.9 = bf16[72,768]{1,0:T(8,128)(2,1)S(1)} fusion(bf16[2240,768]{1,0:T(8,128)(2,1)} %maximum_maximum_fusion), kind=kCustom, calls=%all-reduce-scatter.1 | all-reduce-scatter fusion | flops 1769473 | bytes 3552256
  496.9 15.3 %all-gather.2 = bf16[4,70,640]{2,1,0:T(8,128)(2,1)S(1)} all-gather(bf16[1,70,640]{2,1,0:T(8,128)(2,1)S(1)} %fusion.47), channel_id=1, replica_groups=mesh['y'=4,'zl'=2,'x'=4,'zh'=4,'c'=2] {'x'}, dimensions={0}, use_global_device_ids=true | all-gather | bytes 448000 | tf_op jit(solution)/shard_map/all_gather | solution.py:74
  512.3 8.2 %all_gather.26 = bf16[560,640]{1,0:T(8,128)(2,1)} all-gather(bf16[280,640]{1,0:T(8,128)(2,1)S(1)} %reshape.473), channel_id=1, replica_groups=mesh['y'=4,'zl'=2,'x'=4,'zh'=4,'c'=2] {'zl'}, dimensions={0}, use_global_device_ids=true | all-gather | bytes 1075200 | tf_op jit(solution)/shard_map/all_gather | solution.py:74
  520.6 43.0 %all-gather.8.cloned.1.call-done = bf16[2240,640]{1,0:T(8,128)(2,1)} async-done(((bf16[560,640]{1,0:T(8,128)(2,1)}), bf16[2240,640]{1,0:T(8,128)(2,1)}) %all-gather.8.cloned.1.call-update) | async-done | bytes 2867216 | tf_op jit(solution)/shard_map/all_gather | solution.py:74
  567.9 41.5 %reduce-scatter.8.cloned.1.call-done = bf16[280,160]{1,0:T(8,128)(2,1)} async-done(((bf16[2240,160]{1,0:T(8,128)(2,1)}), bf16[280,160]{1,0:T(8,128)(2,1)}) %reduce-scatter.8.cloned.1.call-update) | async-done | bytes 89616
  (209 shorter events, 94.1 us)
Async XLA Ops:
  7.2 45.3 %copy-start = (bf16[160,896]{1,0:T(8,128)(2,1)S(1)}, bf16[160,896]{1,0:T(8,128)(2,1)}, u32[]{:S(2)}) copy-start(bf16[160,896]{1,0:T(8,128)(2,1)} %param.17) | copy-start | bytes 860164
  7.2 264.3 %all-gather.6.cloned.1.call-start = ((), (), s32[]{:S(2)}) async-start(), calls=%async_computation.1 | async-start | bytes 5017600 | tf_op jit(solution)/shard_map/all_gather | solution.py:74
  57.0 130.1 %copy-start.9 = (s32[5]{0:T(128)S(1)}, s32[5]{0:T(128)}, u32[]{:S(2)}) copy-start(s32[5]{0:T(128)} %param.22) | copy-start | bytes 64
  57.0 130.1 %copy-start.12 = (s32[5]{0:T(128)S(1)}, s32[5]{0:T(128)}, u32[]{:S(2)}) copy-start(s32[5]{0:T(128)} %param.23) | copy-start | bytes 64
  57.0 130.9 %copy-start.11 = (bf16[896]{0:T(1024)(128)(2,1)S(1)}, bf16[896]{0:T(1024)(128)(2,1)}, u32[]{:S(2)}) copy-start(bf16[896]{0:T(1024)(128)(2,1)} %param.18) | copy-start | bytes 5380
  57.0 130.9 %copy-start.15 = (u32[256]{0:T(256)S(1)}, u32[256]{0:T(256)}, u32[]{:S(2)}) copy-start(u32[256]{0:T(256)} %constant.122) | copy-start | bytes 3076
  172.8 25.3 %collective-permute-start = (f32[80,896]{1,0:T(8,128)S(1)}, f32[80,896]{1,0:T(8,128)S(1)}, u32[]{:S(2)}, u32[]{:S(2)}) collective-permute-start(f32[80,896]{1,0:T(8,128)S(1)} %fusion.8), channel_id=1, source_target_pairs={{0,8},{8,16},{16,24},{24,32},{32,40},{40,48},{48,56},{56,64},{64,7... | collective-permute-start | bytes 860168
  175.0 23.2 %collective-permute-start.1 = (f32[80,896]{1,0:T(8,128)S(1)}, f32[80,896]{1,0:T(8,128)S(1)}, u32[]{:S(2)}, u32[]{:S(2)}) collective-permute-start(f32[80,896]{1,0:T(8,128)S(1)} %fusion.8), channel_id=1, source_target_pairs={{0,16},{8,24},{16,32},{24,40},{32,48},{40,56},{48,64},{56,72},{64,... | collective-permute-start | bytes 860168
  178.4 19.7 %collective-permute-start.2 = (f32[80,896]{1,0:T(8,128)S(1)}, f32[80,896]{1,0:T(8,128)S(1)}, u32[]{:S(2)}, u32[]{:S(2)}) collective-permute-start(f32[80,896]{1,0:T(8,128)S(1)} %fusion.8), channel_id=1, source_target_pairs={{0,24},{8,32},{16,40},{24,48},{32,56},{40,64},{48,72},{56,80},{64,... | collective-permute-start | bytes 860168
  183.7 14.5 %collective-permute-start.3 = (f32[70,896]{1,0:T(8,128)S(1)}, f32[70,896]{1,0:T(8,128)S(1)}, u32[]{:S(2)}, u32[]{:S(2)}) collective-permute-start(f32[70,896]{1,0:T(8,128)S(1)} %slice.63), channel_id=1, source_target_pairs={{0,32},{8,40},{16,48},{24,56},{32,64},{40,72},{48,80},{56,88},{64,... | collective-permute-start | bytes 752648
  224.7 338.9 %all-gather.8.cloned.1.call-start = ((), (), s32[]{:S(2)}) async-start(), calls=%async_computation.2 | async-start | bytes 3584000 | tf_op jit(solution)/shard_map/all_gather | solution.py:74
  271.5 1.8 slice-start
  278.5 4.8 copy-start.1
  283.4 6.7 %copy-start.3 = (bf16[5,272,128]{2,1,0:T(8,128)(2,1)S(1)}, bf16[5,272,128]{2,1,0:T(8,128)(2,1)}, u32[]{:S(2)}) copy-start(bf16[5,272,128]{2,1,0:T(8,128)(2,1)} %param.20) | copy-start | bytes 1044484
  283.4 6.7 %copy-start.4 = (bf16[5,272,128]{2,1,0:T(8,128)(2,1)S(1)}, bf16[5,272,128]{2,1,0:T(8,128)(2,1)}, u32[]{:S(2)}) copy-start(bf16[5,272,128]{2,1,0:T(8,128)(2,1)} %param.21) | copy-start | bytes 1044484
  286.7 4.0 copy-start.8
  286.8 4.0 copy-start.10
  286.8 4.0 copy-start.13
  392.3 4.3 copy-start.5
  401.2 90.5 %copy-start.14 = (s32[70]{0:T(128)S(1)}, s32[70]{0:T(128)}, u32[]{:S(2)}) copy-start(s32[70]{0:T(128)} %get-tuple-element.234) | copy-start | bytes 844
  489.6 74.0 %copy-start.7 = (bf16[640,160]{0,1:T(8,128)(2,1)S(1)}, bf16[640,160]{0,1:T(8,128)(2,1)}, u32[]{:S(2)}) copy-start(bf16[640,160]{0,1:T(8,128)(2,1)} %param.19) | copy-start | bytes 614404
  489.7 6.6 %collective-permute-start.4 = (bf16[62,768]{1,0:T(8,128)(2,1)S(1)}, bf16[62,768]{1,0:T(8,128)(2,1)S(1)}, u32[]{:S(2)}, u32[]{:S(2)}) collective-permute-start(bf16[62,768]{1,0:T(8,128)(2,1)S(1)} %slice.64), channel_id=1, source_target_pairs={{0,8},{8,16},{16,24},{24,32},{32,40},{40,48},{48,56},{56,64},{64,7... | collective-permute-start | bytes 285704
  520.5 88.9 %reduce-scatter.8.cloned.1.call-start = ((), (), s32[]{:S(2)}) async-start(), calls=%async_computation.3 | async-start | bytes 1290240
  566.4 44.0 %copy-start.2 = (bf16[280,160]{0,1:T(8,128)(2,1)S(1)}, bf16[280,160]{0,1:T(8,128)(2,1)}, u32[]{:S(2)}) copy-start(bf16[280,160]{0,1:T(8,128)(2,1)} %param.15) | copy-start | bytes 268804
  (1 other events, 0.7 us)
Sparse Core Ops, SparseCore 0:
  224.8 46.6 all-gather.5
  520.7 42.8 all-gather.7
  568.0 41.3 reduce-scatter.7
where the time goes:
time: 619 us; the launch traced here: 618 us
  blocking collectives  332 us (54%)
  waiting for transfers between devices  144 us (23%)
  local copies, waits for them, and re-layouts  48.8 us (8%)
  matrix products  32.1 us (5%)
  other arithmetic  16.9 us (3%)
  starting transfers between devices  16.4 us (3%)
  between operations  15.6 us (3%)
  loops' own time  12.7 us (2%)
    unnamed x2, blocking collectives  204 us
    all_gather x2, waiting for transfers between devices, gather_gx(): value = lax.all_gather(value, axis, axis=0, tiled=True)  89.4 us
    unnamed x9, waiting for transfers between devices  54.2 us
    all_gather x4, blocking collectives, gather_gx(): value = lax.all_gather(value, axis, axis=0, tiled=True)  47.6 us
    pmax x3, blocking collectives, pmax_gx(): value = lax.pmax(value, axis)  37.6 us
    psum x3, blocking collectives, psum_gx(): value = lax.psum(value, axis)  23 us
    dot_general x10, matrix products, scores_for(): jnp.einsum('ikgd,pkd->kgip', query_req, key_req, preferred_element_type=j...  19.2 us
    all_gather x1, blocking collectives, per_device(): gathered = lax.all_gather(normed, GY, axis=0, tiled=True)  19.2 us
  transfers between devices with their start and end apart: 8, of which 5 were waited for; matrix products, arithmetic and copies ran while one was open for 0% of the time, Pallas kernels for 0%

commit v1 on v0

--- a/solution.py
+++ b/solution.py
@@ -77,7 +77,7 @@
 
 def psum_gx(value):
     for axis in GX[::-1]:
-        value = lax.psum(value, axis)
+        value = jnp.sum(lax.all_gather(value, axis), axis=0)
     return value
 
 

time: 619 us -> 628 us (1.015)
    unnamed x2 -> x5, blocking collectives: 204 us -> 227 us
    psum x3 -> x0, blocking collectives: 23 us -> none  [psum_gx(): value = lax.psum(value, axis)]
    unnamed x49 -> x58, local copies, waits for them, and re-layouts: 11.2 us -> 15.9 us
where the time goes in v1:
time: 628 us; the launch traced here: 626 us
  blocking collectives  332 us (53%)
  waiting for transfers between devices  143 us (23%)
  local copies, waits for them, and re-layouts  54.6 us (9%)
  matrix products  32.1 us (5%)
  between operations  17.7 us (3%)
  other arithmetic  16.9 us (3%)
  starting transfers between devices  16.5 us (3%)
  loops' own time  14 us (2%)
    unnamed x5, blocking collectives  227 us
    all_gather x2, waiting for transfers between devices, gather_gx(): value = lax.all_gather(value, axis, axis=0, tiled=True)  88.9 us
    unnamed x9, waiting for transfers between devices  53.8 us
    all_gather x4, blocking collectives, gather_gx(): value = lax.all_gather(value, axis, axis=0, tiled=True)  47.7 us
    pmax x3, blocking collectives, pmax_gx(): value = lax.pmax(value, axis)  37.6 us
    dot_general x10, matrix products, scores_for(): jnp.einsum('ikgd,pkd->kgip', query_req, key_req, preferred_element_type=j...  19.2 us
    all_gather x1, blocking collectives, per_device(): gathered = lax.all_gather(normed, GY, axis=0, tiled=True)  19.2 us
    unnamed x6, starting transfers between devices  16.4 us
  transfers between devices with their start and end apart: 8, of which 5 were waited for; matrix products, arithmetic and copies ran while one was open for 0% of the time, Pallas kernels for 0%

profile of v1, /device:TPU:10, one launch (start us, length us, event | category | flops | bytes accessed | tf_op | source)
XLA Modules:
  0.0 626.5 jit_solution(1323620775198033264)
XLA Ops:
  10.4 8.7 %all-reduce = f32[1120]{0:T(1024)S(1)} all-reduce(f32[1120]{0:T(1024)S(1)} %dynamic-update-slice), channel_id=2, replica_groups=mesh['y'=4,'zl'=2,'x'=4,'zh'=4,'c'=2] {'x'}, use_global_device_ids=true, to_apply=%add | all-reduce | flops 1120 | bytes 8960
  21.4 4.9 all-reduce.1
  28.6 9.6 %all-reduce.2 = f32[1120]{0:T(1024)S(1)} all-reduce(f32[1120]{0:T(1024)S(1)} %dynamic-update-slice.2), channel_id=4, replica_groups=mesh['y'=4,'zl'=2,'x'=4,'zh'=4,'c'=2] {'y'}, use_global_device_ids=true, to_apply=%add.2 | all-reduce | flops 1120 | bytes 8960
  39.4 19.2 %all-gather.3 = bf16[8,280,160]{1,2,0:T(8,128)(2,1)S(1)} all-gather(bf16[1,280,160]{1,2,0:T(8,128)(2,1)S(1)} %fusion.46), channel_id=1, replica_groups=mesh['y'=4,'zl'=2,'x'=4,'zh'=4,'c'=2] {'zh','c'}, dimensions={0}, use_global_device_ids=true | all-gather | bytes 806400 | tf_op jit(solution)/shard_map/all_gather | solution.py:121
  59.6 4.5 fusion.63
  64.1 115.8 %fusion.8 = f32[80,896]{1,0:T(8,128)S(1)} fusion(f32[2240,896]{1,0:T(8,128)} %fusion.63), kind=kCustom, calls=%all-reduce-scatter | all-reduce-scatter fusion | flops 2293761 | bytes 8315904
  185.5 5.3 collective-permute-start.2
  196.7 8.5 %collective-permute-done.3 = f32[70,896]{1,0:T(8,128)S(1)} collective-permute-done((f32[70,896]{1,0:T(8,128)S(1)}, f32[70,896]{1,0:T(8,128)S(1)}, u32[]{:S(2)}, u32[]{:S(2)}) %collective-permute-start.3) | collective-permute-done | bytes 250912
  207.4 14.5 %all-gather.4 = bf16[4,70,896]{2,1,0:T(8,128)(2,1)S(1)} all-gather(bf16[1,70,896]{2,1,0:T(8,128)(2,1)S(1)} %maximum_bitcast_fusion.1), channel_id=1, replica_groups=mesh['y'=4,'zl'=2,'x'=4,'zh'=4,'c'=2] {'x'}, dimensions={0}, use_global_device_ids=true | all-gather | bytes 627200 | tf_op jit(solution)/shard_map/all_gather | solution.py:74
  222.1 9.7 %all_gather.47 = bf16[560,896]{1,0:T(8,128)(2,1)} all-gather(bf16[280,896]{1,0:T(8,128)(2,1)S(1)} %reshape.487), channel_id=1, replica_groups=mesh['y'=4,'zl'=2,'x'=4,'zh'=4,'c'=2] {'zl'}, dimensions={0}, use_global_device_ids=true | all-gather | bytes 1505280 | tf_op jit(solution)/shard_map/all_gather | solution.py:74
  232.3 45.9 %all-gather.9.cloned.1.call-done = bf16[2240,896]{1,0:T(8,128)(2,1)} async-done(((bf16[560,896]{1,0:T(8,128)(2,1)}), bf16[2240,896]{1,0:T(8,128)(2,1)}) %all-gather.9.cloned.1.call-update) | async-done | bytes 4014096 | tf_op jit(solution)/shard_map/all_gather | solution.py:74
  280.0 5.2 reshape.449
  285.2 4.8 copy.68
  297.4 25.9 %while.24 = (s32[]{:T(128)}, bf16[5,1,5,448]{3,2,1,0:T(8,128)(2,1)S(1)}, s32[5]{0:T(128)S(1)}, s32[5]{0:T(128)S(1)}, bf16[5,272,1,128]{3,1,2,0:T(8,128)(2,1)S(1)...) while((s32[]{:T(128)}, bf16[5,1,5,448]{3,2,1,0:T(8,128)(2,1)S(1)}, ...), condition=%wide.region_9.11_spmd.clone, body=%wide.region_7.10_spmd.clone.sunk | while | flops 158046256 | bytes 932525 | solution.py:159
  323.3 14.4 %pmax.21 = bf16[5,1,5,448]{3,2,1,0:T(8,128)(2,1)S(1)} all-reduce(bf16[5,1,5,448]{3,2,1,0:T(8,128)(2,1)S(1)} %get-tuple-element.104), channel_id=1, replica_groups=mesh['y'=4,'zl'=2,'x'=4,'zh'=4,'c'=2] {'x'}, use_global_device_ids=true, to_apply=%region_10.12 | all-reduce | flops 11200 | bytes 44800 | tf_op jit(solution)/shard_map/pmax | solution.py:86
  337.7 8.6 %pmax.22 = bf16[5,1,5,448]{3,2,1,0:T(8,128)(2,1)S(1)} all-reduce(bf16[5,1,5,448]{3,2,1,0:T(8,128)(2,1)S(1)} %pmax.21), channel_id=1, replica_groups=mesh['y'=4,'zl'=2,'x'=4,'zh'=4,'c'=2] {'zl'}, use_global_device_ids=true, to_apply=%region_11.13 | all-reduce | flops 11200 | bytes 44800 | tf_op jit(solution)/shard_map/pmax | solution.py:86
  346.2 14.7 %pmax.23 = bf16[5,1,5,448]{3,2,1,0:T(8,128)(2,1)S(1)} all-reduce(bf16[5,1,5,448]{3,2,1,0:T(8,128)(2,1)S(1)} %pmax.22), channel_id=1, replica_groups=mesh['y'=4,'zl'=2,'x'=4,'zh'=4,'c'=2] {'y'}, use_global_device_ids=true, to_apply=%region_12.14 | all-reduce | flops 11200 | bytes 44800 | tf_op jit(solution)/shard_map/pmax | solution.py:86
  361.0 39.4 %while.25 = (s32[]{:T(128)}, bf16[5,448,640]{1,2,0:T(8,128)(2,1)}, bf16[5,448,5]{1,2,0:T(8,128)(2,1)S(1)}, bf16[5,272,1,128]{3,1,2,0:T(8,128)(2,1)S(1)}, s32[5]{...) while((s32[]{:T(128)}, bf16[5,448,640]{1,2,0:T(8,128)(2,1)}, ...), condition=%wide.region_15.17_spmd.clone, body=%wide.region_13.16_spmd.clone.sunk | while | flops 318286912 | bytes 9364173 | solution.py:176
  401.1 4.3 copy.69
  410.1 88.4 %fusion.9 = bf16[72,768]{1,0:T(8,128)(2,1)S(1)} fusion(bf16[2240,768]{1,0:T(8,128)(2,1)} %maximum_maximum_fusion), kind=kCustom, calls=%all-reduce-scatter.1 | all-reduce-scatter fusion | flops 1769473 | bytes 3552256
  505.8 15.3 %all-gather.5 = bf16[4,70,640]{2,1,0:T(8,128)(2,1)S(1)} all-gather(bf16[1,70,640]{2,1,0:T(8,128)(2,1)S(1)} %fusion.47), channel_id=1, replica_groups=mesh['y'=4,'zl'=2,'x'=4,'zh'=4,'c'=2] {'x'}, dimensions={0}, use_global_device_ids=true | all-gather | bytes 448000 | tf_op jit(solution)/shard_map/all_gather | solution.py:74
  521.2 8.2 %all_gather.50 = bf16[560,640]{1,0:T(8,128)(2,1)} all-gather(bf16[280,640]{1,0:T(8,128)(2,1)S(1)} %reshape.489), channel_id=1, replica_groups=mesh['y'=4,'zl'=2,'x'=4,'zh'=4,'c'=2] {'zl'}, dimensions={0}, use_global_device_ids=true | all-gather | bytes 1075200 | tf_op jit(solution)/shard_map/all_gather | solution.py:74
  529.5 43.1 %all-gather.11.cloned.1.call-done = bf16[2240,640]{1,0:T(8,128)(2,1)} async-done(((bf16[560,640]{1,0:T(8,128)(2,1)}), bf16[2240,640]{1,0:T(8,128)(2,1)}) %all-gather.11.cloned.1.call-update) | async-done | bytes 2867216 | tf_op jit(solution)/shard_map/all_gather | solution.py:74
  576.8 41.4 %reduce-scatter.8.cloned.1.call-done = bf16[280,160]{1,0:T(8,128)(2,1)} async-done(((bf16[2240,160]{1,0:T(8,128)(2,1)}), bf16[280,160]{1,0:T(8,128)(2,1)}) %reduce-scatter.8.cloned.1.call-update) | async-done | bytes 89616
  (224 shorter events, 99.9 us)
Async XLA Ops:
  7.2 52.5 %copy-start = (bf16[160,896]{1,0:T(8,128)(2,1)S(1)}, bf16[160,896]{1,0:T(8,128)(2,1)}, u32[]{:S(2)}) copy-start(bf16[160,896]{1,0:T(8,128)(2,1)} %param.17) | copy-start | bytes 860164
  7.2 271.0 %all-gather.9.cloned.1.call-start = ((), (), s32[]{:S(2)}) async-start(), calls=%async_computation.1 | async-start | bytes 5017600 | tf_op jit(solution)/shard_map/all_gather | solution.py:74
  64.1 130.2 %copy-start.9 = (s32[5]{0:T(128)S(1)}, s32[5]{0:T(128)}, u32[]{:S(2)}) copy-start(s32[5]{0:T(128)} %param.22) | copy-start | bytes 64
  64.1 130.2 %copy-start.12 = (s32[5]{0:T(128)S(1)}, s32[5]{0:T(128)}, u32[]{:S(2)}) copy-start(s32[5]{0:T(128)} %param.23) | copy-start | bytes 64
  64.1 130.9 %copy-start.11 = (bf16[896]{0:T(1024)(128)(2,1)S(1)}, bf16[896]{0:T(1024)(128)(2,1)}, u32[]{:S(2)}) copy-start(bf16[896]{0:T(1024)(128)(2,1)} %param.18) | copy-start | bytes 5380
  64.1 130.9 %copy-start.15 = (u32[256]{0:T(256)S(1)}, u32[256]{0:T(256)}, u32[]{:S(2)}) copy-start(u32[256]{0:T(256)} %constant.140) | copy-start | bytes 3076
  179.9 25.2 %collective-permute-start = (f32[80,896]{1,0:T(8,128)S(1)}, f32[80,896]{1,0:T(8,128)S(1)}, u32[]{:S(2)}, u32[]{:S(2)}) collective-permute-start(f32[80,896]{1,0:T(8,128)S(1)} %fusion.8), channel_id=1, source_target_pairs={{0,8},{8,16},{16,24},{24,32},{32,40},{40,48},{48,56},{56,64},{64,7... | collective-permute-start | bytes 860168
  182.1 23.1 %collective-permute-start.1 = (f32[80,896]{1,0:T(8,128)S(1)}, f32[80,896]{1,0:T(8,128)S(1)}, u32[]{:S(2)}, u32[]{:S(2)}) collective-permute-start(f32[80,896]{1,0:T(8,128)S(1)} %fusion.8), channel_id=1, source_target_pairs={{0,16},{8,24},{16,32},{24,40},{32,48},{40,56},{48,64},{56,72},{64,... | collective-permute-start | bytes 860168
  185.5 19.7 %collective-permute-start.2 = (f32[80,896]{1,0:T(8,128)S(1)}, f32[80,896]{1,0:T(8,128)S(1)}, u32[]{:S(2)}, u32[]{:S(2)}) collective-permute-start(f32[80,896]{1,0:T(8,128)S(1)} %fusion.8), channel_id=1, source_target_pairs={{0,24},{8,32},{16,40},{24,48},{32,56},{40,64},{48,72},{56,80},{64,... | collective-permute-start | bytes 860168
  190.8 14.3 %collective-permute-start.3 = (f32[70,896]{1,0:T(8,128)S(1)}, f32[70,896]{1,0:T(8,128)S(1)}, u32[]{:S(2)}, u32[]{:S(2)}) collective-permute-start(f32[70,896]{1,0:T(8,128)S(1)} %slice.63), channel_id=1, source_target_pairs={{0,32},{8,40},{16,48},{24,56},{32,64},{40,72},{48,80},{56,88},{64,... | collective-permute-start | bytes 752648
  231.9 340.6 %all-gather.11.cloned.1.call-start = ((), (), s32[]{:S(2)}) async-start(), calls=%async_computation.2 | async-start | bytes 3584000 | tf_op jit(solution)/shard_map/all_gather | solution.py:74
  278.2 1.8 slice-start
  285.2 4.8 copy-start.1
  290.1 6.7 %copy-start.3 = (bf16[5,272,128]{2,1,0:T(8,128)(2,1)S(1)}, bf16[5,272,128]{2,1,0:T(8,128)(2,1)}, u32[]{:S(2)}) copy-start(bf16[5,272,128]{2,1,0:T(8,128)(2,1)} %param.20) | copy-start | bytes 1044484
  290.1 6.7 %copy-start.4 = (bf16[5,272,128]{2,1,0:T(8,128)(2,1)S(1)}, bf16[5,272,128]{2,1,0:T(8,128)(2,1)}, u32[]{:S(2)}) copy-start(bf16[5,272,128]{2,1,0:T(8,128)(2,1)} %param.21) | copy-start | bytes 1044484
  293.4 4.0 copy-start.8
  293.4 4.0 copy-start.10
  293.4 4.0 copy-start.13
  401.1 4.3 copy-start.5
  410.1 90.5 %copy-start.14 = (s32[70]{0:T(128)S(1)}, s32[70]{0:T(128)}, u32[]{:S(2)}) copy-start(s32[70]{0:T(128)} %get-tuple-element.234) | copy-start | bytes 844
  498.6 73.9 %copy-start.7 = (bf16[640,160]{0,1:T(8,128)(2,1)S(1)}, bf16[640,160]{0,1:T(8,128)(2,1)}, u32[]{:S(2)}) copy-start(bf16[640,160]{0,1:T(8,128)(2,1)} %param.19) | copy-start | bytes 614404
  498.6 6.6 %collective-permute-start.4 = (bf16[62,768]{1,0:T(8,128)(2,1)S(1)}, bf16[62,768]{1,0:T(8,128)(2,1)S(1)}, u32[]{:S(2)}, u32[]{:S(2)}) collective-permute-start(bf16[62,768]{1,0:T(8,128)(2,1)S(1)} %slice.64), channel_id=1, source_target_pairs={{0,8},{8,16},{16,24},{24,32},{32,40},{40,48},{48,56},{56,64},{64,7... | collective-permute-start | bytes 285704
  529.4 88.8 %reduce-scatter.8.cloned.1.call-start = ((), (), s32[]{:S(2)}) async-start(), calls=%async_computation.3 | async-start | bytes 1290240
  575.3 43.9 %copy-start.2 = (bf16[280,160]{0,1:T(8,128)(2,1)S(1)}, bf16[280,160]{0,1:T(8,128)(2,1)}, u32[]{:S(2)}) copy-start(bf16[280,160]{0,1:T(8,128)(2,1)} %param.15) | copy-start | bytes 268804
  (1 other events, 0.7 us)
Sparse Core Ops, SparseCore 0:
  232.0 46.1 all-gather.8
  529.5 42.9 all-gather.10
  576.9 41.2 reduce-scatter.7
